TPU v7x, 256 devices: a whole 4x4x8 slice. The times are simulated.
256 devices in a mesh: track: 64 (over y, z, core), det: 4 (over x).
Axes of the slice: x: 4, y: 4, z: 8, core: 2. Of those that a mesh axis runs over, the one named last changes fastest.
Arguments:
- jac: float32 [32768, 12, 512], P('track', None, 'det'), may hold values from -1.75 to 1.75
- obs: float32 [32768, 512], P('track', 'det'), may hold values from -6 to 6
- match: int32 [32768], P('track'), may hold values from 0 to 32767, as said below
- tile_knot: int32 [32768], P('track'), may hold values from 0 to 127
- tile_frac: float32 [32768], P('track'), may hold values from 0 to 1
Outputs:
- knot_field: float32 [12, 8192], P(None, 'track')
- tie_residual: float32 [32768, 512], P('track', 'det')
Inputs may be any that keep to these rules, and one draw needn't show every extreme that they name: match[match[i]] = i and match[i] != i; the tiles of each index of track cross exactly 8 tiles of every index of track, itself included.
All inputs are finite; a program needn't handle non-finite values.
Results may differ from a plain program's by a relative error of at most 0.0001.
Values sent between devices are 32-bit elements; how exact they have to be, the bound alone decides.
A program may use at most 64 MiB of HBM per device.

v0:
```python
import jax
import jax.numpy as jnp
from jax import lax
from jax.sharding import PartitionSpec as P

KNOT_DEV = 128
ITERS = 4
damping = 1.0


def passed_along(value, axis, steps):
    count = lax.axis_size(axis)
    leading, last = (max(0, -steps), min(count, count - steps))
    return lax.ppermute(value, axis, [(source, source + steps) for source in range(leading, last)])


def local(jac, obs, match, tile_knot, tile_frac):
    highest = lax.Precision.HIGHEST
    tiles_dev = jac.shape[0]
    params = jac.shape[1]
    n_track = lax.axis_size("track")
    n_det = lax.axis_size("det")
    per_peer = tiles_dev // n_track
    send_order = jnp.argsort(match // tiles_dev, stable=True)

    def arrange(values):
        return values[send_order].reshape((n_track, per_peer) + values.shape[1:])

    slots_in = lax.all_to_all(
        arrange(match % tiles_dev), "track", split_axis=0, concat_axis=0, tiled=True
    )
    receive_order = jnp.argsort(slots_in.reshape(-1))

    def settle(arrived):
        joined = arrived.reshape((tiles_dev,) + arrived.shape[2:])
        return joined[receive_order]

    def partner_values(values):
        return settle(
            lax.all_to_all(arrange(values), "track", split_axis=0, concat_axis=0, tiled=True)
        )

    knot_rows = lax.broadcasted_iota(jnp.int32, (KNOT_DEV, tiles_dev), 0)
    weights = jnp.where(knot_rows == tile_knot[None, :], 1.0 - tile_frac[None, :], 0.0)
    weights = weights + jnp.where(knot_rows == tile_knot[None, :] + 1, tile_frac[None, :], 0.0)
    weights_back = weights.T
    edge_weight = jnp.where(tile_knot == KNOT_DEV - 1, tile_frac, 0.0)
    misfit = obs - partner_values(obs)

    def adjoint(residual_rows):
        partial_value = jnp.einsum("ipw,iw->pi", jac, residual_rows, precision=highest)
        partial_value = lax.psum(partial_value, "det")
        spread = jnp.dot(partial_value, weights_back, precision=highest)
        spill_over = jnp.dot(partial_value, edge_weight, precision=highest)
        carried = passed_along(spill_over, "track", 1)
        return spread.at[:, 0].add(carried)

    def slope_total(gradient):
        return lax.psum(jnp.sum(gradient * gradient), "track")

    knot_field = jnp.zeros((params, KNOT_DEV), jnp.float32)
    tie_residual = misfit
    gradient = adjoint(tie_residual)
    direction = gradient
    slope_norm = slope_total(gradient)
    for iteration in range(ITERS):
        following = passed_along(direction[:, 0], "track", -1)
        interp = (
            jnp.dot(direction, weights, precision=highest)
            + following[:, None] * edge_weight[None, :]
        )
        own_pred = jnp.einsum("ipw,pi->iw", jac, interp, precision=highest)
        other_pred = partner_values(own_pred)
        change = own_pred - other_pred
        change_sq, direction_sq = lax.psum(
            (jnp.sum(change * change), jnp.sum(direction * direction)), ("track", "det")
        )
        curvature = 0.5 * change_sq + damping * direction_sq / n_det
        step_length = slope_norm / curvature
        knot_field = knot_field + step_length * direction
        tie_residual = tie_residual - step_length * change
        gradient = adjoint(tie_residual) - damping * knot_field
        new_norm = slope_total(gradient)
        direction = gradient + new_norm / slope_norm * direction
        slope_norm = new_norm
    return (knot_field, tie_residual)


def solution(mesh):
    in_specs = (P("track", None, "det"), P("track", "det"), P("track"), P("track"), P("track"))
    out_specs = (P(None, "track"), P("track", "det"))
    return jax.shard_map(local, mesh=mesh, in_specs=in_specs, out_specs=out_specs, check_vma=False)
```

profile of v0, /device:TPU:1, one launch (start us, length us, event | category | flops | bytes accessed | tf_op | source)
XLA Modules:
  0.0 1151.5 jit_solution(3248454608757837504)
XLA Ops:
  9.5 13.1 %all-to-all-start.1 = ((s32[64,1,8]{2,1,0:T(1,128)}), s32[64,1,8]{2,1,0:T(1,128)S(1)}, u32[]{:S(2)}, u32[]{:S(2)}) async-start(s32[64,1,8]{2,1,0:T(1,128)} %bitcast.2), calls=%async_computation.1 | async-start | bytes 65536 | tf_op jit(solution)/shard_map/all_to_all | solution.py:29
  25.7 6.2 all-to-all-done.1
  42.6 6.8 all-to-all-done
  53.7 7.9 fusion.14
  61.6 16.9 %psum.112 = f32[12,512]{0,1:T(8,128)} all-reduce(f32[12,512]{0,1:T(8,128)S(1)} %bitcast.110), channel_id=1, replica_groups=mesh['track'=64,'det'=4] {'det'}, use_global_device_ids=true, to_apply=%region_2.3 | all-reduce | flops 6144 | bytes 49152 | tf_op jit(solution)/shard_map/psum | solution.py:52
  79.7 7.5 collective-permute-start
  95.8 6.3 fusion.12
  103.7 9.0 all-to-all-start.2
  113.4 124.9 %psum.113 = f32[]{:T(128)} all-reduce(f32[]{:T(128)} %multiply_reduce_fusion.10), channel_id=1, replica_groups=mesh['track'=64,'det'=4] {'track'}, use_global_device_ids=true, to_apply=%region_5.6 | all-reduce | flops 1 | bytes 8 | tf_op jit(solution)/shard_map/psum | solution.py:59
  243.2 75.6 %all-reduce.3 = (f32[]{:T(128)}, f32[]{:T(128)}) all-reduce(f32[]{:T(128)} %get-tuple-element.77, f32[]{:T(128)} %multiply_reduce_fusion.10), channel_id=1, replica_groups=mesh['track'=64,'det'=4] {'track','det'}, use_global_device_ids=true, to_apply=%region_7.8 | all-reduce | flops 2 | bytes 16 | tf_op jit(solution)/shard_map/psum | solution.py:75
  322.5 7.9 fusion.10
  330.4 16.5 %psum.116 = f32[12,512]{0,1:T(8,128)} all-reduce(f32[12,512]{0,1:T(8,128)S(1)} %bitcast.111), channel_id=1, replica_groups=mesh['track'=64,'det'=4] {'det'}, use_global_device_ids=true, to_apply=%region_9.10 | all-reduce | flops 6144 | bytes 49152 | tf_op jit(solution)/shard_map/psum | solution.py:52
  349.6 8.1 collective-permute-start.2
  359.8 121.8 %psum.117 = f32[]{:T(128)} all-reduce(f32[]{:T(128)} %multiply_reduce_fusion.9), channel_id=1, replica_groups=mesh['track'=64,'det'=4] {'track'}, use_global_device_ids=true, to_apply=%region_11.12 | all-reduce | flops 1 | bytes 8 | tf_op jit(solution)/shard_map/psum | solution.py:59
  490.8 6.3 fusion.8
  498.8 17.1 %all_to_all.34 = f32[64,8,128]{2,1,0:T(8,128)} all-to-all(f32[64,8,128]{2,1,0:T(8,128)} %bitcast.117), channel_id=1, replica_groups=mesh['track'=64,'det'=4] {'track'}, dimensions={0} | all-to-all | bytes 524288 | tf_op jit(solution)/shard_map/all_to_all | solution.py:40
  520.9 75.0 %all-reduce.2 = (f32[]{:T(128)}, f32[]{:T(128)}) all-reduce(f32[]{:T(128)} %get-tuple-element.75, f32[]{:T(128)} %get-tuple-element.73), channel_id=1, replica_groups=mesh['track'=64,'det'=4] {'track','det'}, use_global_device_ids=true, to_apply=%region_13.14 | all-reduce | flops 2 | bytes 16 | tf_op jit(solution)/shard_map/psum | solution.py:75
  599.5 7.9 fusion.6
  607.4 15.1 %psum.120 = f32[12,512]{0,1:T(8,128)} all-reduce(f32[12,512]{0,1:T(8,128)S(1)} %bitcast.112), channel_id=1, replica_groups=mesh['track'=64,'det'=4] {'det'}, use_global_device_ids=true, to_apply=%region_16.17 | all-reduce | flops 6144 | bytes 49152 | tf_op jit(solution)/shard_map/psum | solution.py:52
  625.1 8.4 collective-permute-start.4
  635.7 121.8 %psum.121 = f32[]{:T(128)} all-reduce(f32[]{:T(128)} %get-tuple-element.70), channel_id=1, replica_groups=mesh['track'=64,'det'=4] {'track'}, use_global_device_ids=true, to_apply=%region_18.19 | all-reduce | flops 1 | bytes 8 | tf_op jit(solution)/shard_map/psum | solution.py:59
  759.5 5.7 collective-permute-start.5
  766.7 6.3 fusion.4
  774.7 17.2 %all_to_all.35 = f32[64,8,128]{2,1,0:T(8,128)} all-to-all(f32[64,8,128]{2,1,0:T(8,128)} %bitcast.118), channel_id=1, replica_groups=mesh['track'=64,'det'=4] {'track'}, dimensions={0} | all-to-all | bytes 524288 | tf_op jit(solution)/shard_map/all_to_all | solution.py:40
  796.8 74.7 %all-reduce.1 = (f32[]{:T(128)}, f32[]{:T(128)}) all-reduce(f32[]{:T(128)} %get-tuple-element.68, f32[]{:T(128)} %get-tuple-element.66), channel_id=1, replica_groups=mesh['track'=64,'det'=4] {'track','det'}, use_global_device_ids=true, to_apply=%region_20.21 | all-reduce | flops 2 | bytes 16 | tf_op jit(solution)/shard_map/psum | solution.py:75
  875.1 7.9 fusion.2
  883.0 15.2 %psum.124 = f32[12,512]{0,1:T(8,128)} all-reduce(f32[12,512]{0,1:T(8,128)S(1)} %bitcast.113), channel_id=1, replica_groups=mesh['track'=64,'det'=4] {'det'}, use_global_device_ids=true, to_apply=%region_23.24 | all-reduce | flops 6144 | bytes 49152 | tf_op jit(solution)/shard_map/psum | solution.py:52
  900.9 8.5 collective-permute-start.6
  911.6 121.8 %psum.125 = f32[]{:T(128)} all-reduce(f32[]{:T(128)} %multiply_reduce_fusion.5), channel_id=1, replica_groups=mesh['track'=64,'det'=4] {'track'}, use_global_device_ids=true, to_apply=%region_25.26 | all-reduce | flops 1 | bytes 8 | tf_op jit(solution)/shard_map/psum | solution.py:59
  1042.7 6.3 fusion
  1050.7 17.2 %all_to_all.36 = f32[64,8,128]{2,1,0:T(8,128)} all-to-all(f32[64,8,128]{2,1,0:T(8,128)} %bitcast.116), channel_id=1, replica_groups=mesh['track'=64,'det'=4] {'track'}, dimensions={0} | all-to-all | bytes 524288 | tf_op jit(solution)/shard_map/all_to_all | solution.py:40
  1072.8 74.3 %all-reduce = (f32[]{:T(128)}, f32[]{:T(128)}) all-reduce(f32[]{:T(128)} %get-tuple-element.64, f32[]{:T(128)} %get-tuple-element.62), channel_id=1, replica_groups=mesh['track'=64,'det'=4] {'track','det'}, use_global_device_ids=true, to_apply=%region_27.28 | all-reduce | flops 2 | bytes 16 | tf_op jit(solution)/shard_map/psum | solution.py:75
  (104 shorter events, 103.7 us)
Async XLA Ops:
  0.6 53.1 %copy-start = (f32[512,12,128]{2,0,1:T(8,128)S(1)}, f32[512,12,128]{2,0,1:T(8,128)}, u32[]{:S(2)}) copy-start(f32[512,12,128]{2,0,1:T(8,128)} %param.13) | copy-start | bytes 9437188
  0.6 36.8 %copy-start.6 = (s32[512]{0:T(512)S(1)}, s32[512]{0:T(512)}, u32[]{:S(2)}) copy-start(s32[512]{0:T(512)} %param.16) | copy-start | bytes 6148
  0.7 22.7 %copy-start.1 = (f32[512,128]{1,0:T(8,128)S(1)}, f32[512,128]{1,0:T(8,128)}, u32[]{:S(2)}) copy-start(f32[512,128]{1,0:T(8,128)} %param.14) | copy-start | bytes 786436
  9.5 22.5 %all-to-all-start.1 = ((s32[64,1,8]{2,1,0:T(1,128)}), s32[64,1,8]{2,1,0:T(1,128)S(1)}, u32[]{:S(2)}, u32[]{:S(2)}) async-start(s32[64,1,8]{2,1,0:T(1,128)} %bitcast.2), calls=%async_computation.1 | async-start | bytes 65536 | tf_op jit(solution)/shard_map/all_to_all | solution.py:29
  32.0 17.4 %all-to-all-start = ((f32[64,8,128]{2,1,0:T(8,128)}), f32[64,8,128]{2,1,0:T(8,128)}, u32[]{:S(2)}, u32[]{:S(2)}) async-start(f32[64,8,128]{2,1,0:T(8,128)} %bitcast.114), calls=%async_computation | async-start | bytes 524288 | tf_op jit(solution)/shard_map/all_to_all | solution.py:40
  52.0 35.2 %copy-start.7 = (f32[512]{0:T(512)S(1)}, f32[512]{0:T(512)}, u32[]{:S(2)}) copy-start(f32[512]{0:T(512)} %param.17) | copy-start | bytes 6148
  53.0 0.7 copy-start.2
  79.7 9.0 collective-permute-start
  89.7 4.9 collective-permute-start.1
  103.7 134.6 %all-to-all-start.2 = ((f32[64,8,128]{2,1,0:T(8,128)}), f32[64,8,128]{2,1,0:T(8,128)}, u32[]{:S(2)}, u32[]{:S(2)}) async-start(f32[64,8,128]{2,1,0:T(8,128)} %bitcast.115), calls=%async_computation.2 | async-start | bytes 524288 | tf_op jit(solution)/shard_map/all_to_all | solution.py:40
  321.8 0.7 copy-start.5
  349.6 8.8 collective-permute-start.2
  483.7 6.0 collective-permute-start.3
  598.8 0.7 copy-start.4
  625.1 9.1 collective-permute-start.4
  759.5 6.0 collective-permute-start.5
  874.4 0.7 copy-start.3
  900.9 9.2 collective-permute-start.6
  1035.6 6.0 collective-permute-start.7
where the time goes:
time: 1160 us; the launch traced here: 1150 us
  blocking collectives  905 us (78%)
  starting transfers between devices  78.6 us (7%)
  matrix products  68.8 us (6%)
  other arithmetic  33.7 us (3%)
  local copies, waits for them, and re-layouts  33.2 us (3%)
  waiting for transfers between devices  19.6 us (2%)
  between operations  12.4 us (1%)
    psum x4, blocking collectives, slope_total(): return lax.psum(jnp.sum(gradient * gradient), 'track')  490 us
    psum x4, blocking collectives, local(): lax.psum((jnp.sum(change * change), jnp.sum(direction * direction)), ('tr...  300 us
    psum x4, blocking collectives, adjoint(): partial_value = lax.psum(partial_value, 'det')  63.7 us
    all_to_all x3, blocking collectives, partner_values(): lax.all_to_all(arrange(values), 'track', split_axis=0, concat_axis=0, til...  51.5 us
    ppermute x8, starting transfers between devices, passed_along(): lax.ppermute(value, axis, [(source, source + steps) for source in range(l...  51 us
    dot_general x4, matrix products, adjoint(): jnp.einsum('ipw,iw->pi', jac, residual_rows, precision=highest)  31.6 us
    dot_general x4, matrix products, local(): own_pred = jnp.einsum('ipw,pi->iw', jac, interp, precision=highest)  25.3 us
  transfers between devices with their start and end apart: 11, of which 9 were waited for; matrix products, arithmetic and copies ran while one was open for 1% of the time, Pallas kernels for 0%

commit v1 on v0

--- a/solution.py
+++ b/solution.py
@@ -49,7 +49,8 @@
 
     def adjoint(residual_rows):
         partial_value = jnp.einsum("ipw,iw->pi", jac, residual_rows, precision=highest)
-        partial_value = lax.psum(partial_value, "det")
+        parts = lax.all_gather(partial_value, "det")
+        partial_value = jnp.sum(parts, axis=0)
         spread = jnp.dot(partial_value, weights_back, precision=highest)
         spill_over = jnp.dot(partial_value, edge_weight, precision=highest)
         carried = passed_along(spill_over, "track", 1)

time: 1160 us -> 1130 us (0.974)
  blocking collectives: 905 us -> 882 us
    psum x4 -> x0, blocking collectives: 63.7 us -> none  [adjoint(): partial_value = lax.psum(partial_value, 'det')]
    all_gather x0 -> x4, blocking collectives: none -> 37.4 us  [adjoint(): parts = lax.all_gather(partial_value, 'det')]
  transfers between devices with their start and end apart: 11 -> 11, of which waited for: 9 -> 10; matrix products, arithmetic and copies ran while one was open for 1% -> 1% of each run, Pallas kernels for 0% -> 0%
where the time goes in v1:
time: 1130 us; the launch traced here: 1120 us
  blocking collectives  882 us (78%)
  starting transfers between devices  74.3 us (7%)
  matrix products  59.7 us (5%)
  other arithmetic  33.8 us (3%)
  local copies, waits for them, and re-layouts  33.7 us (3%)
  waiting for transfers between devices  20.5 us (2%)
  between operations  12.3 us (1%)
    psum x4, blocking collectives, slope_total(): return lax.psum(jnp.sum(gradient * gradient), 'track')  493 us
    psum x4, blocking collectives, local(): lax.psum((jnp.sum(change * change), jnp.sum(direction * direction)), ('tr...  300 us
    all_to_all x3, blocking collectives, partner_values(): lax.all_to_all(arrange(values), 'track', split_axis=0, concat_axis=0, til...  51.4 us
    ppermute x8, starting transfers between devices, passed_along(): lax.ppermute(value, axis, [(source, source + steps) for source in range(l...  46.6 us
    all_gather x4, blocking collectives, adjoint(): parts = lax.all_gather(partial_value, 'det')  37.4 us
    dot_general x4, matrix products, adjoint(): jnp.einsum('ipw,iw->pi', jac, residual_rows, precision=highest)  31.6 us
    dot_general x4, matrix products, local(): own_pred = jnp.einsum('ipw,pi->iw', jac, interp, precision=highest)  25.3 us
  transfers between devices with their start and end apart: 11, of which 10 were waited for; matrix products, arithmetic and copies ran while one was open for 1% of the time, Pallas kernels for 0%

profile of v1, /device:TPU:1, one launch (start us, length us, event | category | flops | bytes accessed | tf_op | source)
XLA Modules:
  0.0 1116.4 jit_solution(16090305261838818245)
XLA Ops:
  9.5 13.1 %all-to-all-start.1 = ((s32[64,1,8]{2,1,0:T(1,128)}), s32[64,1,8]{2,1,0:T(1,128)S(1)}, u32[]{:S(2)}, u32[]{:S(2)}) async-start(s32[64,1,8]{2,1,0:T(1,128)} %bitcast.2), calls=%async_computation.1 | async-start | bytes 65536 | tf_op jit(solution)/shard_map/all_to_all | solution.py:29
  25.7 6.2 all-to-all-done.1
  42.6 6.8 all-to-all-done
  53.7 7.9 fusion.14
  61.7 9.9 all-gather.4
  71.8 6.3 collective-permute-start
  86.3 6.3 fusion.12
  94.3 9.1 all-to-all-start.2
  104.0 124.9 %psum.84 = f32[]{:T(128)} all-reduce(f32[]{:T(128)} %multiply_reduce_fusion.10), channel_id=1, replica_groups=mesh['track'=64,'det'=4] {'track'}, use_global_device_ids=true, to_apply=%region_5.6 | all-reduce | flops 1 | bytes 8 | tf_op jit(solution)/shard_map/psum | solution.py:60
  233.8 77.9 %all-reduce.3 = (f32[]{:T(128)}, f32[]{:T(128)}) all-reduce(f32[]{:T(128)} %get-tuple-element.77, f32[]{:T(128)} %multiply_reduce_fusion.10), channel_id=1, replica_groups=mesh['track'=64,'det'=4] {'track','det'}, use_global_device_ids=true, to_apply=%region_7.8 | all-reduce | flops 2 | bytes 16 | tf_op jit(solution)/shard_map/psum | solution.py:76
  315.4 7.9 fusion.10
  323.4 9.1 all-gather.5
  332.9 7.6 collective-permute-start.2
  342.7 121.8 %psum.87 = f32[]{:T(128)} all-reduce(f32[]{:T(128)} %multiply_reduce_fusion.9), channel_id=1, replica_groups=mesh['track'=64,'det'=4] {'track'}, use_global_device_ids=true, to_apply=%region_11.12 | all-reduce | flops 1 | bytes 8 | tf_op jit(solution)/shard_map/psum | solution.py:60
  473.7 6.3 fusion.8
  481.7 17.1 %all_to_all.34 = f32[64,8,128]{2,1,0:T(8,128)} all-to-all(f32[64,8,128]{2,1,0:T(8,128)} %bitcast.117), channel_id=1, replica_groups=mesh['track'=64,'det'=4] {'track'}, dimensions={0} | all-to-all | bytes 524288 | tf_op jit(solution)/shard_map/all_to_all | solution.py:40
  503.8 74.6 %all-reduce.2 = (f32[]{:T(128)}, f32[]{:T(128)}) all-reduce(f32[]{:T(128)} %get-tuple-element.75, f32[]{:T(128)} %get-tuple-element.73), channel_id=1, replica_groups=mesh['track'=64,'det'=4] {'track','det'}, use_global_device_ids=true, to_apply=%region_13.14 | all-reduce | flops 2 | bytes 16 | tf_op jit(solution)/shard_map/psum | solution.py:76
  582.0 7.9 fusion.6
  590.0 9.2 all-gather.6
  599.7 7.1 collective-permute-start.4
  609.0 122.8 %psum.90 = f32[]{:T(128)} all-reduce(f32[]{:T(128)} %get-tuple-element.70), channel_id=1, replica_groups=mesh['track'=64,'det'=4] {'track'}, use_global_device_ids=true, to_apply=%region_18.19 | all-reduce | flops 1 | bytes 8 | tf_op jit(solution)/shard_map/psum | solution.py:60
  733.8 5.7 collective-permute-start.5
  741.0 6.3 fusion.4
  749.0 17.1 %all_to_all.35 = f32[64,8,128]{2,1,0:T(8,128)} all-to-all(f32[64,8,128]{2,1,0:T(8,128)} %bitcast.118), channel_id=1, replica_groups=mesh['track'=64,'det'=4] {'track'}, dimensions={0} | all-to-all | bytes 524288 | tf_op jit(solution)/shard_map/all_to_all | solution.py:40
  771.1 73.8 %all-reduce.1 = (f32[]{:T(128)}, f32[]{:T(128)}) all-reduce(f32[]{:T(128)} %get-tuple-element.68, f32[]{:T(128)} %get-tuple-element.66), channel_id=1, replica_groups=mesh['track'=64,'det'=4] {'track','det'}, use_global_device_ids=true, to_apply=%region_20.21 | all-reduce | flops 2 | bytes 16 | tf_op jit(solution)/shard_map/psum | solution.py:76
  848.4 7.9 fusion.2
  856.4 9.2 all-gather.7
  866.1 7.1 collective-permute-start.6
  875.4 123.7 %psum.93 = f32[]{:T(128)} all-reduce(f32[]{:T(128)} %multiply_reduce_fusion.5), channel_id=1, replica_groups=mesh['track'=64,'det'=4] {'track'}, use_global_device_ids=true, to_apply=%region_25.26 | all-reduce | flops 1 | bytes 8 | tf_op jit(solution)/shard_map/psum | solution.py:60
  1008.3 6.3 fusion
  1016.3 17.2 %all_to_all.36 = f32[64,8,128]{2,1,0:T(8,128)} all-to-all(f32[64,8,128]{2,1,0:T(8,128)} %bitcast.116), channel_id=1, replica_groups=mesh['track'=64,'det'=4] {'track'}, dimensions={0} | all-to-all | bytes 524288 | tf_op jit(solution)/shard_map/all_to_all | solution.py:40
  1038.4 73.6 %all-reduce = (f32[]{:T(128)}, f32[]{:T(128)}) all-reduce(f32[]{:T(128)} %get-tuple-element.64, f32[]{:T(128)} %get-tuple-element.62), channel_id=1, replica_groups=mesh['track'=64,'det'=4] {'track','det'}, use_global_device_ids=true, to_apply=%region_27.28 | all-reduce | flops 2 | bytes 16 | tf_op jit(solution)/shard_map/psum | solution.py:76
  (112 shorter events, 96.2 us)
Async XLA Ops:
  0.6 53.1 %copy-start = (f32[512,12,128]{2,0,1:T(8,128)S(1)}, f32[512,12,128]{2,0,1:T(8,128)}, u32[]{:S(2)}) copy-start(f32[512,12,128]{2,0,1:T(8,128)} %param.13) | copy-start | bytes 9437188
  0.6 36.8 %copy-start.6 = (s32[512]{0:T(512)S(1)}, s32[512]{0:T(512)}, u32[]{:S(2)}) copy-start(s32[512]{0:T(512)} %param.16) | copy-start | bytes 6148
  0.7 22.7 %copy-start.1 = (f32[512,128]{1,0:T(8,128)S(1)}, f32[512,128]{1,0:T(8,128)}, u32[]{:S(2)}) copy-start(f32[512,128]{1,0:T(8,128)} %param.14) | copy-start | bytes 786436
  9.5 22.5 %all-to-all-start.1 = ((s32[64,1,8]{2,1,0:T(1,128)}), s32[64,1,8]{2,1,0:T(1,128)S(1)}, u32[]{:S(2)}, u32[]{:S(2)}) async-start(s32[64,1,8]{2,1,0:T(1,128)} %bitcast.2), calls=%async_computation.1 | async-start | bytes 65536 | tf_op jit(solution)/shard_map/all_to_all | solution.py:29
  32.0 17.4 %all-to-all-start = ((f32[64,8,128]{2,1,0:T(8,128)}), f32[64,8,128]{2,1,0:T(8,128)}, u32[]{:S(2)}, u32[]{:S(2)}) async-start(f32[64,8,128]{2,1,0:T(8,128)} %bitcast.114), calls=%async_computation | async-start | bytes 524288 | tf_op jit(solution)/shard_map/all_to_all | solution.py:40
  52.0 26.1 %copy-start.7 = (f32[512]{0:T(512)S(1)}, f32[512]{0:T(512)}, u32[]{:S(2)}) copy-start(f32[512]{0:T(512)} %param.17) | copy-start | bytes 6148
  53.0 0.7 copy-start.2
  71.8 7.0 collective-permute-start
  79.7 5.4 collective-permute-start.1
  94.3 134.7 %all-to-all-start.2 = ((f32[64,8,128]{2,1,0:T(8,128)}), f32[64,8,128]{2,1,0:T(8,128)}, u32[]{:S(2)}, u32[]{:S(2)}) async-start(f32[64,8,128]{2,1,0:T(8,128)} %bitcast.115), calls=%async_computation.2 | async-start | bytes 524288 | tf_op jit(solution)/shard_map/all_to_all | solution.py:40
  314.6 0.7 copy-start.5
  332.9 8.3 collective-permute-start.2
  466.5 6.0 collective-permute-start.3
  581.3 0.7 copy-start.4
  599.7 7.8 collective-permute-start.4
  733.8 6.1 collective-permute-start.5
  847.7 0.7 copy-start.3
  866.1 7.8 collective-permute-start.6
  1001.1 6.1 collective-permute-start.7
